TPU v7x, 32 devices: a whole 2x2x4 slice. The times are simulated.
32 devices in a mesh: grp: 4 (over y, x), mem: 8 (over z, core).
Axes of the slice: x: 2, y: 2, z: 4, core: 2. Of those that a mesh axis runs over, the one named last changes fastest.
Arguments:
- factors: bfloat16 [32, 512, 2048], P(('grp', 'mem')), may hold values from -1 to 1
- occ_energy: bfloat16 [32], P(('grp', 'mem')), may hold values from -1.5 to -0.29882812
- vir_energy: bfloat16 [512], replicated, may hold values from 0.3984375 to 3
- pair_code: int32 [4, 8, 3], P('grp'), may hold values from 0 to 2
- pair_count: int32 [4, 8], P('grp'), may hold values from 1 to 3
Outputs:
- aux_density: bfloat16 [32, 512, 2048], P(('grp', 'mem'))
- lagrangian: bfloat16 [32, 512, 2048], P(('grp', 'mem'))
Inputs may be any that keep to these rules, and one draw needn't show every extreme that they name: `pair_code`: only the first pair_count entries of a device's list are read; entries may repeat.
All inputs are finite; a program needn't handle non-finite values.
Results may differ from a plain program's by a relative error of at most 0.0056.
Values may be sent and summed in bfloat16 or wider, within the bound.
No kernel may reach another device: no remote copies, remote signals or barrier semaphores. Data moves between devices by JAX's collectives and lax.ppermute only.
A program may use at most 128 MiB of HBM per device.

v0:
```python
import jax
import jax.numpy as jnp
from jax import lax
from jax.sharding import PartitionSpec as P

OCC_DEV = 1
ROUNDS = 2


def partner(value, axis, distance):
    mask = 2**distance
    pairs = [(source, source ^ mask) for source in range(lax.axis_size(axis))]
    return lax.ppermute(value, axis, pairs)


def decode_pair(code):
    round_no = code // (OCC_DEV * OCC_DEV)
    left_orb = code // OCC_DEV % OCC_DEV
    right_orb = code % OCC_DEV
    return (round_no, left_orb, right_orb)


def add_at(target, indices, contribution):
    zero_index = jnp.zeros((), jnp.int32)
    anchor = tuple(indices) + (zero_index,) * contribution.ndim
    extent = (1,) * len(indices) + contribution.shape
    current = lax.dynamic_slice(target, anchor, extent)
    return lax.dynamic_update_slice(target, current + contribution.reshape(extent), anchor)


def outer_terms(amp_tile):
    return lax.dot_general(
        amp_tile, amp_tile, (((1,), (1,)), ((), ())), preferred_element_type=jnp.float32
    )


def near_product(amp_tile, right_block):
    return jnp.dot(amp_tile, right_block, preferred_element_type=jnp.float32)


def far_product(amp_tile, left_block):
    return lax.dot_general(
        amp_tile, left_block, (((0,), (0,)), ((), ())), preferred_element_type=jnp.float32
    )


def per_device(factors, occ_energy, vir_energy, pair_code, pair_count):
    virtual = vir_energy.astype(jnp.float32)
    my_place = lax.axis_index("mem")
    group_codes = pair_code[0]
    group_counts = pair_count[0]
    my_codes = lax.dynamic_index_in_dim(group_codes, my_place, 0, keepdims=False)
    live_count = lax.dynamic_index_in_dim(group_counts, my_place, 0, keepdims=False)
    blocks_all = [factors]
    energy_list = [occ_energy]
    for round_idx in range(ROUNDS):
        visitor, visitor_energy = partner((factors, occ_energy), "mem", round_idx)
        blocks_all.append(visitor)
        energy_list.append(visitor_energy)
    stacked = jnp.stack(blocks_all)
    energy_all = jnp.stack(energy_list).astype(jnp.float32)
    vir_count = factors.shape[1]
    density_zero = jnp.zeros((vir_count, vir_count), jnp.float32)

    def pair_terms(slot_no):
        round_no, left_orb, right_orb = decode_pair(my_codes[slot_no])
        left_block = stacked[0, left_orb]
        right_block = stacked[round_no, right_orb]
        integrals = lax.dot_general(
            left_block, right_block, (((1,), (1,)), ((), ())), preferred_element_type=jnp.float32
        )
        denominator = (
            virtual[:, None]
            + virtual[None, :]
            - energy_all[0, left_orb]
            - energy_all[round_no, right_orb]
        )
        amp_tile = (integrals / denominator).astype(jnp.bfloat16)
        return (round_no, left_orb, right_orb, left_block, right_block, amp_tile)

    def pair_step(slot_no, carry_pair):
        density, totals = carry_pair
        round_no, left_orb, right_orb, left_block, right_block, amp_tile = pair_terms(slot_no)
        density = density + outer_terms(amp_tile)
        totals = add_at(
            totals, (jnp.zeros((), jnp.int32), left_orb), near_product(amp_tile, right_block)
        )
        totals = add_at(totals, (round_no, right_orb), far_product(amp_tile, left_block))
        return (density, totals)

    totals_zero = jnp.zeros((ROUNDS + 1,) + factors.shape, jnp.float32)
    density, totals = lax.fori_loop(0, live_count, pair_step, (density_zero, totals_zero))
    gathered = totals[0]
    for round_idx in range(ROUNDS):
        gathered = gathered + partner(totals[round_idx + 1], "mem", round_idx)
    density = lax.psum(density, "mem")
    density = lax.psum(density, "grp")
    density_scale = 1.0 / (8.0 * lax.axis_size("grp") * lax.axis_size("mem"))
    density_tile = (density * density_scale).astype(jnp.bfloat16)
    lagrangian = jnp.einsum(
        "ab,kbp->kap", density_tile, factors, preferred_element_type=jnp.float32
    )
    return (gathered.astype(jnp.bfloat16), lagrangian.astype(jnp.bfloat16))


def solution(mesh):
    in_specs = (
        P(("grp", "mem"), None, None),
        P(("grp", "mem")),
        P(),
        P("grp", None, None),
        P("grp", None),
    )
    out_specs = (P(("grp", "mem"), None, None), P(("grp", "mem"), None, None))
    return jax.shard_map(
        per_device, mesh=mesh, in_specs=in_specs, out_specs=out_specs, check_vma=False
    )
```

profile of v0, /device:TPU:0, one launch (start us, length us, event | category | flops | bytes accessed | tf_op | source)
XLA Modules:
  0.0 274.6 jit_solution(6055429350554140018)
XLA Ops:
  7.2 0.0 copy-start
  7.2 0.0 all-reduce.3.cloned.1.call-start
  7.2 0.6 collective-permute-start
  7.8 2.6 collective-permute-start.1
  10.4 0.1 collective-permute-start.3
  10.5 0.1 collective-permute-start.2
  11.3 0.7 convert_element_type.38
  11.9 1.2 constant_dynamic-slice_fusion.1
  13.2 0.2 dynamic-slice_reduce_fusion
  13.4 43.7 %collective-permute-done.3 = bf16[1]{0:T(256)(128)(2,1)} collective-permute-done((bf16[1]{0:T(256)(128)(2,1)}, bf16[1]{0:T(256)(128)(2,1)}, u32[]{:S(2)}, u32[]{:S(2)}) %collective-permute-start.3) | collective-permute-done | bytes 34 | tf_op jit(solution)/shard_map/ppermute | solution.py:13
  57.1 0.0 collective-permute-done.2
  57.1 1.3 maximum_convert_fusion
  58.3 0.0 collective-permute-done
  58.3 0.0 collective-permute-done.1
  58.3 5.5 %pad_maximum_fusion = bf16[3,1,512,2048]{3,2,1,0:T(8,128)(2,1)} fusion(bf16[1,1,512,2048]{3,2,1,0:T(8,128)(2,1)} %bitcast.11, bf16[1,1,512,2048]{3,2,1,0:T(8,128)(2,1)S(1)} %bitcast.93, bf16[1,1,512,2048]{3,2,1,0:T(8,128)(2,1)} %bitcast.92), kind=kLoop, calls=%fused_computation.19 | loop fusion | flops 6291456 | bytes 12582912 | tf_op jit(solution)/shard_map/stack | solution.py:60
  63.8 0.1 broadcast_in_dim.8
  63.9 6.1 %broadcast_in_dim.9 = f32[3,1,512,2048]{3,2,1,0:T(8,128)} broadcast(f32[]{:T(128)} %constant.74.clone.1), dimensions={} | broadcast | bytes 12582916 | tf_op jit(solution)/shard_map/broadcast_in_dim | solution.py:91
  70.1 39.3 %while.14 = (s32[]{:T(128)}, f32[512,512]{1,0:T(8,128)S(1)}, f32[3,1,512,2048]{3,2,1,0:T(8,128)}, s32[]{:T(128)}, s32[3]{0:T(128)S(1)}, /*index=5*/bf16[3,1,512,...) while((s32[]{:T(128)}, f32[512,512]{1,0:T(8,128)S(1)}, ...), condition=%wide.region_1.2_spmd, body=%wide.region_0.1_spmd.sunk | while | flops 3493330944 | bytes 155194704 | solution.py:92
  70.7 0.6 dynamic_slice.94
  73.4 0.6 fusion.52
  74.0 6.0 %divide_convert_fusion.2 = bf16[512,512]{0,1:T(8,128)(2,1)S(1)} fusion(bf16[3,1,512,2048]{3,2,1,0:T(8,128)(2,1)} %get-tuple-element.212, s32[]{:T(128)S(6)} %select_n.46, f32[]{:T(128)} %bitcast.89, f32[]{:T(128)} %bitcast.90, f32[512]{0:T(512)S(1)} %get-tuple-element.213), kind=kOutput, calls=%fused_computation.15.clone.1 | convolution fusion | flops 1075052544 | bytes 4723716 | tf_op jit(solution)/shard_map/while/body/dot_general | solution.py:69
  80.0 0.5 convolution_add_fusion.2
  80.5 1.1 copy-done.3
  81.7 1.6 fusion.53
  83.2 1.6 fusion.54
  84.9 4.5 %copy-done.2 = f32[3,1,512,2048]{3,2,1,0:T(8,128)} copy-done((f32[3,1,512,2048]{3,2,1,0:T(8,128)}, f32[3,1,512,2048]{3,2,1,0:T(8,128)S(1)}, u32[]{:S(2)}) %copy-start.2) | copy-done | bytes 12582936 | tf_op jit(solution)/shard_map/while
  90.1 0.6 dynamic_slice.94
  92.7 0.6 fusion.52
  93.4 6.0 %divide_convert_fusion.2 = bf16[512,512]{0,1:T(8,128)(2,1)S(1)} fusion(bf16[3,1,512,2048]{3,2,1,0:T(8,128)(2,1)} %get-tuple-element.212, s32[]{:T(128)S(6)} %select_n.46, f32[]{:T(128)} %bitcast.89, f32[]{:T(128)} %bitcast.90, f32[512]{0:T(512)S(1)} %get-tuple-element.213), kind=kOutput, calls=%fused_computation.15.clone.1 | convolution fusion | flops 1075052544 | bytes 4723716 | tf_op jit(solution)/shard_map/while/body/dot_general | solution.py:69
  99.4 0.5 convolution_add_fusion.2
  99.9 1.1 copy-done.3
  101.0 1.6 fusion.53
  102.6 1.6 fusion.54
  104.2 4.5 %copy-done.2 = f32[3,1,512,2048]{3,2,1,0:T(8,128)} copy-done((f32[3,1,512,2048]{3,2,1,0:T(8,128)}, f32[3,1,512,2048]{3,2,1,0:T(8,128)S(1)}, u32[]{:S(2)}) %copy-start.2) | copy-done | bytes 12582936 | tf_op jit(solution)/shard_map/while
  109.4 0.0 copy-start.4
  109.4 0.0 copy-start.5
  109.4 8.2 %slice_bitcast_fusion.1 = (f32[1,512,2048]{2,1,0:T(8,128)}, f32[1,512,2048]{2,1,0:T(8,128)}) fusion(f32[3,1,512,2048]{3,2,1,0:T(8,128)} %get-tuple-element.109), kind=kLoop, calls=%fused_computation.24 | loop fusion | bytes 16777216 | tf_op jit(solution)/shard_map/squeeze | solution.py:95
  117.7 19.1 %collective-permute-start.4 = (f32[1,512,2048]{2,1,0:T(8,128)}, f32[1,512,2048]{2,1,0:T(8,128)}, u32[]{:S(2)}, u32[]{:S(2)}) collective-permute-start(f32[1,512,2048]{2,1,0:T(8,128)} %get-tuple-element.129), channel_id=1, source_target_pairs={{0,1},{1,0},{2,3},{3,2},{4,5},{5,4},{6,7},{7,6},{8,9},{9,8},{10,11... | collective-permute-start | bytes 12582920 | tf_op jit(solution)/shard_map/ppermute | solution.py:13
  136.8 2.0 collective-permute-start.5
  138.8 0.0 all-reduce.3.cloned.1.call-update
  138.8 0.0 all-reduce.5.cloned.1.call-start
  138.8 63.4 %all-reduce.3.cloned.1.call-done = f32[512,512]{1,0:T(8,128)} async-done(((f32[512,512]{1,0:T(8,128)}), f32[512,512]{1,0:T(8,128)}) %all-reduce.3.cloned.1.call-update) | async-done | bytes 1048592 | tf_op jit(solution)/shard_map/psum | solution.py:96
  202.3 0.0 all-reduce.5.cloned.1.call-update
  202.3 54.6 %all-reduce.5.cloned.1.call-done = f32[512,512]{1,0:T(8,128)} async-done(((f32[512,512]{1,0:T(8,128)}), f32[512,512]{1,0:T(8,128)}) %all-reduce.5.cloned.1.call-update) | async-done | bytes 1048592 | tf_op jit(solution)/shard_map/psum | solution.py:97
  256.9 3.8 %fusion.24 = bf16[1,512,2048]{2,1,0:T(8,128)(2,1)} fusion(bf16[1,512,2048]{2,1,0:T(8,128)(2,1)S(1)} %copy-done.5, f32[512,512]{1,0:T(8,128)} %all-reduce.5.cloned.1.call-done), kind=kOutput, calls=%fused_computation.26 | convolution fusion | flops 1075314688 | bytes 5242880 | tf_op jit(solution)/shard_map/ab,kbp->kap/dot_general | solution.py:100
  260.7 0.0 collective-permute-done.4
  260.7 0.0 collective-permute-done.5
  260.7 7.1 %fusion.23 = bf16[1,512,2048]{2,1,0:T(8,128)(2,1)} fusion(f32[1,512,2048]{2,1,0:T(8,128)} %collective-permute-done.5, f32[1,512,2048]{2,1,0:T(8,128)} %collective-permute-done.4, f32[3,1,512,2048]{3,2,1,0:T(8,128)} %get-tuple-element.109), kind=kLoop, calls=%fused_computation.22 | loop fusion | flops 3145728 | bytes 14680064 | tf_op jit(solution)/shard_map/convert_element_type | solution.py:103
  (11 shorter events, 0.0 us)
Async XLA Ops:
  7.2 6.0 %copy-start = (s32[1,8,3]{1,0,2:T(1,128)S(1)}, s32[1,8,3]{1,0,2:T(1,128)}, u32[]{:S(2)}) copy-start(s32[1,8,3]{1,0,2:T(1,128)} %param.10) | copy-start | bytes 292
  7.2 195.1 %all-reduce.3.cloned.1.call-start = ((), (), s32[]{:S(2)}) async-start(), calls=%async_computation | async-start | bytes 2097152 | tf_op jit(solution)/shard_map/psum | solution.py:96
  7.2 51.1 %collective-permute-start = (bf16[1,512,2048]{2,1,0:T(8,128)(2,1)}, bf16[1,512,2048]{2,1,0:T(8,128)(2,1)S(1)}, u32[]{:S(2)}, u32[]{:S(2)}) collective-permute-start(bf16[1,512,2048]{2,1,0:T(8,128)(2,1)} %param.7), channel_id=1, source_target_pairs={{0,1},{1,0},{2,3},{3,2},{4,5},{5,4},{6,7},{7,6},{8,9},{9,8},{10,11... | collective-permute-start | bytes 6291464 | tf_op jit(solution)/shard_map/ppermute | solution.py:13
  7.8 50.5 %collective-permute-start.1 = (bf16[1,512,2048]{2,1,0:T(8,128)(2,1)}, bf16[1,512,2048]{2,1,0:T(8,128)(2,1)}, u32[]{:S(2)}, u32[]{:S(2)}) collective-permute-start(bf16[1,512,2048]{2,1,0:T(8,128)(2,1)} %param.7), channel_id=1, source_target_pairs={{0,2},{1,3},{2,0},{3,1},{4,6},{5,7},{6,4},{7,5},{8,10},{9,11},{10,... | collective-permute-start | bytes 6291464 | tf_op jit(solution)/shard_map/ppermute | solution.py:13
  10.4 46.6 %collective-permute-start.3 = (bf16[1]{0:T(256)(128)(2,1)}, bf16[1]{0:T(256)(128)(2,1)}, u32[]{:S(2)}, u32[]{:S(2)}) collective-permute-start(bf16[1]{0:T(256)(128)(2,1)} %param.8), channel_id=1, source_target_pairs={{0,2},{1,3},{2,0},{3,1},{4,6},{5,7},{6,4},{7,5},{8,10},{9,11},{10,... | collective-permute-start | bytes 14 | tf_op jit(solution)/shard_map/ppermute | solution.py:13
  10.5 46.6 %collective-permute-start.2 = (bf16[1]{0:T(256)(128)(2,1)}, bf16[1]{0:T(256)(128)(2,1)}, u32[]{:S(2)}, u32[]{:S(2)}) collective-permute-start(bf16[1]{0:T(256)(128)(2,1)} %param.8), channel_id=1, source_target_pairs={{0,1},{1,0},{2,3},{3,2},{4,5},{5,4},{6,7},{7,6},{8,9},{9,8},{10,11... | collective-permute-start | bytes 14 | tf_op jit(solution)/shard_map/ppermute | solution.py:13
  74.0 6.5 %copy-start.1 = (f32[3,1,512,2048]{3,2,1,0:T(8,128)S(1)}, f32[3,1,512,2048]{3,2,1,0:T(8,128)}, u32[]{:S(2)}) copy-start(f32[3,1,512,2048]{3,2,1,0:T(8,128)} %get-tuple-element.198) | copy-start | bytes 37748740 | tf_op jit(solution)/shard_map/while
  74.0 7.6 %copy-start.3 = (bf16[3,1,512,2048]{3,2,1,0:T(8,128)(2,1)S(1)}, bf16[3,1,512,2048]{3,2,1,0:T(8,128)(2,1)}, u32[]{:S(2)}) copy-start(bf16[3,1,512,2048]{3,2,1,0:T(8,128)(2,1)} %get-tuple-element.212) | copy-start | bytes 18874372 | tf_op jit(solution)/shard_map/while
  84.9 4.5 %copy-start.2 = (f32[3,1,512,2048]{3,2,1,0:T(8,128)}, f32[3,1,512,2048]{3,2,1,0:T(8,128)S(1)}, u32[]{:S(2)}) copy-start(f32[3,1,512,2048]{3,2,1,0:T(8,128)S(1)} %fusion.54) | copy-start | bytes 37748740 | tf_op jit(solution)/shard_map/while
  93.4 6.5 %copy-start.1 = (f32[3,1,512,2048]{3,2,1,0:T(8,128)S(1)}, f32[3,1,512,2048]{3,2,1,0:T(8,128)}, u32[]{:S(2)}) copy-start(f32[3,1,512,2048]{3,2,1,0:T(8,128)} %get-tuple-element.198) | copy-start | bytes 37748740 | tf_op jit(solution)/shard_map/while
  93.4 7.6 %copy-start.3 = (bf16[3,1,512,2048]{3,2,1,0:T(8,128)(2,1)S(1)}, bf16[3,1,512,2048]{3,2,1,0:T(8,128)(2,1)}, u32[]{:S(2)}) copy-start(bf16[3,1,512,2048]{3,2,1,0:T(8,128)(2,1)} %get-tuple-element.212) | copy-start | bytes 18874372 | tf_op jit(solution)/shard_map/while
  104.2 4.5 %copy-start.2 = (f32[3,1,512,2048]{3,2,1,0:T(8,128)}, f32[3,1,512,2048]{3,2,1,0:T(8,128)S(1)}, u32[]{:S(2)}) copy-start(f32[3,1,512,2048]{3,2,1,0:T(8,128)S(1)} %fusion.54) | copy-start | bytes 37748740 | tf_op jit(solution)/shard_map/while
  109.4 8.3 %copy-start.4 = (f32[512,512]{1,0:T(8,128)}, f32[512,512]{1,0:T(8,128)S(1)}, u32[]{:S(2)}) copy-start(f32[512,512]{1,0:T(8,128)S(1)} %get-tuple-element.110) | copy-start | bytes 3145732
  109.4 147.5 %copy-start.5 = (bf16[1,512,2048]{2,1,0:T(8,128)(2,1)S(1)}, bf16[1,512,2048]{2,1,0:T(8,128)(2,1)}, u32[]{:S(2)}) copy-start(bf16[1,512,2048]{2,1,0:T(8,128)(2,1)} %param.7) | copy-start | bytes 6291460
  117.7 143.0 %collective-permute-start.4 = (f32[1,512,2048]{2,1,0:T(8,128)}, f32[1,512,2048]{2,1,0:T(8,128)}, u32[]{:S(2)}, u32[]{:S(2)}) collective-permute-start(f32[1,512,2048]{2,1,0:T(8,128)} %get-tuple-element.129), channel_id=1, source_target_pairs={{0,1},{1,0},{2,3},{3,2},{4,5},{5,4},{6,7},{7,6},{8,9},{9,8},{10,11... | collective-permute-start | bytes 12582920 | tf_op jit(solution)/shard_map/ppermute | solution.py:13
  136.8 123.9 %collective-permute-start.5 = (f32[1,512,2048]{2,1,0:T(8,128)}, f32[1,512,2048]{2,1,0:T(8,128)}, u32[]{:S(2)}, u32[]{:S(2)}) collective-permute-start(f32[1,512,2048]{2,1,0:T(8,128)} %get-tuple-element.130), channel_id=1, source_target_pairs={{0,2},{1,3},{2,0},{3,1},{4,6},{5,7},{6,4},{7,5},{8,10},{9,11},{10,... | collective-permute-start | bytes 12582920 | tf_op jit(solution)/shard_map/ppermute | solution.py:13
  138.8 118.1 %all-reduce.5.cloned.1.call-start = ((), (), s32[]{:S(2)}) async-start(), calls=%async_computation.1 | async-start | bytes 2097152 | tf_op jit(solution)/shard_map/psum | solution.py:97
Sparse Core Ops, SparseCore 0:
  138.9 63.3 all-reduce.2
  205.3 51.5 all-reduce.4
where the time goes:
time: 275 us
  waiting for transfers between devices  162 us (59%)
  local copies, waits for them, and re-layouts  29.9 us (11%)
  starting transfers between devices  24.5 us (9%)
  matrix products  23.1 us (8%)
  between operations  14.7 us (5%)
  other arithmetic  14.5 us (5%)
  loops' own time  6.11 us (2%)
    psum x1, waiting for transfers between devices, per_device(): density = lax.psum(density, 'mem')  63.4 us
    psum x1, waiting for transfers between devices, per_device(): density = lax.psum(density, 'grp')  54.6 us
    ppermute x6, waiting for transfers between devices, partner(): return lax.ppermute(value, axis, pairs)  43.7 us
    ppermute x6, starting transfers between devices, partner(): return lax.ppermute(value, axis, pairs)  24.4 us
    dot_general x2, matrix products, pair_terms(): lax.dot_general(left_block, right_block, (((1,), (1,)), ((), ())), prefer...  12 us
    while x12, local copies, waits for them, and re-layouts  11.3 us
    squeeze x1, local copies, waits for them, and re-layouts, per_device(): gathered = gathered + partner(totals[round_idx + 1], 'mem', round_idx)  8.24 us
    convert_element_type x1, other arithmetic, per_device(): return (gathered.astype(jnp.bfloat16), lagrangian.astype(jnp.bfloat16))  7.07 us
  transfers between devices with their start and end apart: 8, of which 3 were waited for; matrix products, arithmetic and copies ran while one was open for 3% of the time, Pallas kernels for 0%

commit v1 on v0

--- a/solution.py
+++ b/solution.py
@@ -93,7 +93,9 @@
     gathered = totals[0]
     for round_idx in range(ROUNDS):
         gathered = gathered + partner(totals[round_idx + 1], "mem", round_idx)
-    density = lax.psum(density, "mem")
+    density = density
+    for hop in (1, 2, 4):
+        density = density + lax.ppermute(density, "mem", [(dev, dev ^ hop) for dev in range(8)])
     density = lax.psum(density, "grp")
     density_scale = 1.0 / (8.0 * lax.axis_size("grp") * lax.axis_size("mem"))
     density_tile = (density * density_scale).astype(jnp.bfloat16)

time: 275 us -> 365 us (1.33)
  waiting for transfers between devices: 162 us -> 249 us
    ppermute x0 -> x3, waiting for transfers between devices: none -> 159 us  [per_device(): lax.ppermute(density, 'mem', [(dev, dev ^ hop) for dev in range(8)])]
    psum x1 -> x0, waiting for transfers between devices: 63.4 us -> none  [per_device(): density = lax.psum(density, 'mem')]
    psum x1, waiting for transfers between devices: 54.6 us -> 45.7 us  [per_device(): density = lax.psum(density, 'grp')]
  transfers between devices with their start and end apart: 8 -> 10, of which waited for: 3 -> 5; matrix products, arithmetic and copies ran while one was open for 3% -> 3% of each run, Pallas kernels for 0% -> 0%
where the time goes in v1:
time: 365 us
  waiting for transfers between devices  249 us (68%)
  local copies, waits for them, and re-layouts  29.4 us (8%)
  starting transfers between devices  26.9 us (7%)
  matrix products  23 us (6%)
  other arithmetic  16.2 us (4%)
  between operations  14.8 us (4%)
  loops' own time  5.83 us (2%)
    ppermute x3, waiting for transfers between devices, per_device(): lax.ppermute(density, 'mem', [(dev, dev ^ hop) for dev in range(8)])  159 us
    psum x1, waiting for transfers between devices, per_device(): density = lax.psum(density, 'grp')  45.7 us
    ppermute x6, waiting for transfers between devices, partner(): return lax.ppermute(value, axis, pairs)  43.6 us
    ppermute x6, starting transfers between devices, partner(): return lax.ppermute(value, axis, pairs)  24.2 us
    dot_general x2, matrix products, pair_terms(): lax.dot_general(left_block, right_block, (((1,), (1,)), ((), ())), prefer...  11.9 us
    while x12, local copies, waits for them, and re-layouts  11.5 us
    squeeze x1, local copies, waits for them, and re-layouts, per_device(): gathered = gathered + partner(totals[round_idx + 1], 'mem', round_idx)  7.86 us
  transfers between devices with their start and end apart: 10, of which 5 were waited for; matrix products, arithmetic and copies ran while one was open for 3% of the time, Pallas kernels for 0%

profile of v1, /device:TPU:0, one launch (start us, length us, event | category | flops | bytes accessed | tf_op | source)
XLA Modules:
  0.0 364.8 jit_solution(5782406197727666720)
XLA Ops:
  7.2 0.0 copy-start
  7.2 0.0 all-reduce.2.cloned.1.call-start
  7.2 0.6 collective-permute-start
  7.8 2.6 collective-permute-start.1
  10.4 0.1 collective-permute-start.3
  10.5 0.1 collective-permute-start.2
  11.3 0.7 convert_element_type.38
  11.9 1.2 constant_dynamic-slice_fusion.1
  13.2 0.2 dynamic-slice_reduce_fusion
  13.4 43.6 %collective-permute-done.3 = bf16[1]{0:T(256)(128)(2,1)} collective-permute-done((bf16[1]{0:T(256)(128)(2,1)}, bf16[1]{0:T(256)(128)(2,1)}, u32[]{:S(2)}, u32[]{:S(2)}) %collective-permute-start.3) | collective-permute-done | bytes 34 | tf_op jit(solution)/shard_map/ppermute | solution.py:13
  57.0 1.2 maximum_convert_fusion
  58.2 5.5 %pad_maximum_fusion = bf16[3,1,512,2048]{3,2,1,0:T(8,128)(2,1)} fusion(bf16[1,1,512,2048]{3,2,1,0:T(8,128)(2,1)} %bitcast.11, bf16[1,1,512,2048]{3,2,1,0:T(8,128)(2,1)S(1)} %bitcast.93, bf16[1,1,512,2048]{3,2,1,0:T(8,128)(2,1)} %bitcast.92), kind=kLoop, calls=%fused_computation.19 | loop fusion | flops 6291456 | bytes 12582912 | tf_op jit(solution)/shard_map/stack | solution.py:60
  63.7 0.1 broadcast_in_dim.8
  63.8 6.1 %broadcast_in_dim.9 = f32[3,1,512,2048]{3,2,1,0:T(8,128)} broadcast(f32[]{:T(128)} %constant.74.clone.1), dimensions={} | broadcast | bytes 12582916 | tf_op jit(solution)/shard_map/broadcast_in_dim | solution.py:91
  69.9 38.9 %while.14 = (s32[]{:T(128)}, f32[512,512]{1,0:T(8,128)S(1)}, f32[3,1,512,2048]{3,2,1,0:T(8,128)}, s32[]{:T(128)}, s32[3]{0:T(128)S(1)}, /*index=5*/bf16[3,1,512,...) while((s32[]{:T(128)}, f32[512,512]{1,0:T(8,128)S(1)}, ...), condition=%wide.region_1.2_spmd, body=%wide.region_0.1_spmd.sunk | while | flops 3493330944 | bytes 155194704 | solution.py:92
  70.6 0.6 dynamic_slice.94
  73.1 0.6 fusion.52
  73.7 5.9 %divide_convert_fusion.2 = bf16[512,512]{0,1:T(8,128)(2,1)S(1)} fusion(bf16[3,1,512,2048]{3,2,1,0:T(8,128)(2,1)} %get-tuple-element.212, s32[]{:T(128)S(6)} %select_n.46, f32[]{:T(128)} %bitcast.89, f32[]{:T(128)} %bitcast.90, f32[512]{0:T(512)S(1)} %get-tuple-element.213), kind=kOutput, calls=%fused_computation.15.clone.1 | convolution fusion | flops 1075052544 | bytes 4723716 | tf_op jit(solution)/shard_map/while/body/dot_general | solution.py:69
  79.6 0.5 convolution_add_fusion.2
  80.1 1.2 copy-done.3
  81.3 1.6 fusion.53
  82.9 1.6 fusion.54
  84.5 4.5 %copy-done.2 = f32[3,1,512,2048]{3,2,1,0:T(8,128)} copy-done((f32[3,1,512,2048]{3,2,1,0:T(8,128)}, f32[3,1,512,2048]{3,2,1,0:T(8,128)S(1)}, u32[]{:S(2)}) %copy-start.2) | copy-done | bytes 12582936 | tf_op jit(solution)/shard_map/while
  89.7 0.6 dynamic_slice.94
  92.2 0.6 fusion.52
  92.8 5.9 %divide_convert_fusion.2 = bf16[512,512]{0,1:T(8,128)(2,1)S(1)} fusion(bf16[3,1,512,2048]{3,2,1,0:T(8,128)(2,1)} %get-tuple-element.212, s32[]{:T(128)S(6)} %select_n.46, f32[]{:T(128)} %bitcast.89, f32[]{:T(128)} %bitcast.90, f32[512]{0:T(512)S(1)} %get-tuple-element.213), kind=kOutput, calls=%fused_computation.15.clone.1 | convolution fusion | flops 1075052544 | bytes 4723716 | tf_op jit(solution)/shard_map/while/body/dot_general | solution.py:69
  98.7 0.5 convolution_add_fusion.2
  99.2 1.2 copy-done.3
  100.4 1.6 fusion.53
  102.0 1.6 fusion.54
  103.6 4.5 %copy-done.2 = f32[3,1,512,2048]{3,2,1,0:T(8,128)} copy-done((f32[3,1,512,2048]{3,2,1,0:T(8,128)}, f32[3,1,512,2048]{3,2,1,0:T(8,128)S(1)}, u32[]{:S(2)}) %copy-start.2) | copy-done | bytes 12582936 | tf_op jit(solution)/shard_map/while
  108.8 7.9 %slice_bitcast_fusion.1 = (f32[1,512,2048]{2,1,0:T(8,128)}, f32[1,512,2048]{2,1,0:T(8,128)}) fusion(f32[3,1,512,2048]{3,2,1,0:T(8,128)} %get-tuple-element.109), kind=kLoop, calls=%fused_computation.24 | loop fusion | bytes 16777216 | tf_op jit(solution)/shard_map/squeeze | solution.py:95
  116.7 19.0 %collective-permute-start.4 = (f32[1,512,2048]{2,1,0:T(8,128)}, f32[1,512,2048]{2,1,0:T(8,128)}, u32[]{:S(2)}, u32[]{:S(2)}) collective-permute-start(f32[1,512,2048]{2,1,0:T(8,128)} %get-tuple-element.129), channel_id=1, source_target_pairs={{0,1},{1,0},{2,3},{3,2},{4,5},{5,4},{6,7},{7,6},{8,9},{9,8},{10,11... | collective-permute-start | bytes 12582920 | tf_op jit(solution)/shard_map/ppermute | solution.py:13
  135.6 1.9 collective-permute-start.5
  137.5 0.2 collective-permute-start.6
  137.8 6.4 %collective-permute-done.6 = f32[512,512]{1,0:T(8,128)S(1)} collective-permute-done((f32[512,512]{1,0:T(8,128)S(1)}, f32[512,512]{1,0:T(8,128)S(1)}, u32[]{:S(2)}, u32[]{:S(2)}) %collective-permute-start.6) | collective-permute-done | bytes 1048608 | tf_op jit(solution)/shard_map/ppermute | solution.py:98
  144.1 0.2 add.102
  144.3 2.3 collective-permute-start.7
  146.7 104.8 %collective-permute-done.7 = f32[512,512]{1,0:T(8,128)S(1)} collective-permute-done((f32[512,512]{1,0:T(8,128)S(1)}, f32[512,512]{1,0:T(8,128)S(1)}, u32[]{:S(2)}, u32[]{:S(2)}) %collective-permute-start.7) | collective-permute-done | bytes 1048608 | tf_op jit(solution)/shard_map/ppermute | solution.py:98
  251.5 0.2 add.103
  251.7 0.1 collective-permute-start.8
  251.7 48.2 %collective-permute-done.8 = f32[512,512]{1,0:T(8,128)S(1)} collective-permute-done((f32[512,512]{1,0:T(8,128)S(1)}, f32[512,512]{1,0:T(8,128)S(1)}, u32[]{:S(2)}, u32[]{:S(2)}) %collective-permute-start.8) | collective-permute-done | bytes 1048608 | tf_op jit(solution)/shard_map/ppermute | solution.py:98
  300.0 1.2 add.104
  301.1 0.0 all-reduce.2.cloned.1.call-update
  301.2 0.0 copy-start.4
  301.2 7.2 %fusion.23 = bf16[1,512,2048]{2,1,0:T(8,128)(2,1)} fusion(f32[1,512,2048]{2,1,0:T(8,128)} %collective-permute-done.5, f32[1,512,2048]{2,1,0:T(8,128)} %collective-permute-done.4, f32[3,1,512,2048]{3,2,1,0:T(8,128)} %get-tuple-element.109), kind=kLoop, calls=%fused_computation.22 | loop fusion | flops 3145728 | bytes 14680064 | tf_op jit(solution)/shard_map/convert_element_type | solution.py:105
  308.4 45.7 %all-reduce.2.cloned.1.call-done = f32[512,512]{1,0:T(8,128)} async-done(((f32[512,512]{1,0:T(8,128)}), f32[512,512]{1,0:T(8,128)}) %all-reduce.2.cloned.1.call-update) | async-done | bytes 1048592 | tf_op jit(solution)/shard_map/psum | solution.py:99
  354.1 3.8 %fusion.24 = bf16[1,512,2048]{2,1,0:T(8,128)(2,1)} fusion(bf16[1,512,2048]{2,1,0:T(8,128)(2,1)S(1)} %copy-done.4, f32[512,512]{1,0:T(8,128)} %all-reduce.2.cloned.1.call-done), kind=kOutput, calls=%fused_computation.26 | convolution fusion | flops 1075314688 | bytes 5242880 | tf_op jit(solution)/shard_map/ab,kbp->kap/dot_general | solution.py:102
  (15 shorter events, 0.0 us)
Async XLA Ops:
  7.2 6.0 %copy-start = (s32[1,8,3]{1,0,2:T(1,128)S(1)}, s32[1,8,3]{1,0,2:T(1,128)}, u32[]{:S(2)}) copy-start(s32[1,8,3]{1,0,2:T(1,128)} %param.10) | copy-start | bytes 292
  7.2 346.9 %all-reduce.2.cloned.1.call-start = ((), (), s32[]{:S(2)}) async-start(), calls=%async_computation | async-start | bytes 2097152 | tf_op jit(solution)/shard_map/psum | solution.py:99
  7.2 51.0 %collective-permute-start = (bf16[1,512,2048]{2,1,0:T(8,128)(2,1)}, bf16[1,512,2048]{2,1,0:T(8,128)(2,1)S(1)}, u32[]{:S(2)}, u32[]{:S(2)}) collective-permute-start(bf16[1,512,2048]{2,1,0:T(8,128)(2,1)} %param.7), channel_id=1, source_target_pairs={{0,1},{1,0},{2,3},{3,2},{4,5},{5,4},{6,7},{7,6},{8,9},{9,8},{10,11... | collective-permute-start | bytes 6291464 | tf_op jit(solution)/shard_map/ppermute | solution.py:13
  7.8 50.4 %collective-permute-start.1 = (bf16[1,512,2048]{2,1,0:T(8,128)(2,1)}, bf16[1,512,2048]{2,1,0:T(8,128)(2,1)}, u32[]{:S(2)}, u32[]{:S(2)}) collective-permute-start(bf16[1,512,2048]{2,1,0:T(8,128)(2,1)} %param.7), channel_id=1, source_target_pairs={{0,2},{1,3},{2,0},{3,1},{4,6},{5,7},{6,4},{7,5},{8,10},{9,11},{10,... | collective-permute-start | bytes 6291464 | tf_op jit(solution)/shard_map/ppermute | solution.py:13
  10.4 46.5 %collective-permute-start.3 = (bf16[1]{0:T(256)(128)(2,1)}, bf16[1]{0:T(256)(128)(2,1)}, u32[]{:S(2)}, u32[]{:S(2)}) collective-permute-start(bf16[1]{0:T(256)(128)(2,1)} %param.8), channel_id=1, source_target_pairs={{0,2},{1,3},{2,0},{3,1},{4,6},{5,7},{6,4},{7,5},{8,10},{9,11},{10,... | collective-permute-start | bytes 14 | tf_op jit(solution)/shard_map/ppermute | solution.py:13
  10.5 46.5 %collective-permute-start.2 = (bf16[1]{0:T(256)(128)(2,1)}, bf16[1]{0:T(256)(128)(2,1)}, u32[]{:S(2)}, u32[]{:S(2)}) collective-permute-start(bf16[1]{0:T(256)(128)(2,1)} %param.8), channel_id=1, source_target_pairs={{0,1},{1,0},{2,3},{3,2},{4,5},{5,4},{6,7},{7,6},{8,9},{9,8},{10,11... | collective-permute-start | bytes 14 | tf_op jit(solution)/shard_map/ppermute | solution.py:13
  73.7 6.4 %copy-start.1 = (f32[3,1,512,2048]{3,2,1,0:T(8,128)S(1)}, f32[3,1,512,2048]{3,2,1,0:T(8,128)}, u32[]{:S(2)}) copy-start(f32[3,1,512,2048]{3,2,1,0:T(8,128)} %get-tuple-element.198) | copy-start | bytes 37748740 | tf_op jit(solution)/shard_map/while
  73.7 7.6 %copy-start.3 = (bf16[3,1,512,2048]{3,2,1,0:T(8,128)(2,1)S(1)}, bf16[3,1,512,2048]{3,2,1,0:T(8,128)(2,1)}, u32[]{:S(2)}) copy-start(bf16[3,1,512,2048]{3,2,1,0:T(8,128)(2,1)} %get-tuple-element.212) | copy-start | bytes 18874372 | tf_op jit(solution)/shard_map/while
  84.5 4.5 %copy-start.2 = (f32[3,1,512,2048]{3,2,1,0:T(8,128)}, f32[3,1,512,2048]{3,2,1,0:T(8,128)S(1)}, u32[]{:S(2)}) copy-start(f32[3,1,512,2048]{3,2,1,0:T(8,128)S(1)} %fusion.54) | copy-start | bytes 37748740 | tf_op jit(solution)/shard_map/while
  92.8 6.4 %copy-start.1 = (f32[3,1,512,2048]{3,2,1,0:T(8,128)S(1)}, f32[3,1,512,2048]{3,2,1,0:T(8,128)}, u32[]{:S(2)}) copy-start(f32[3,1,512,2048]{3,2,1,0:T(8,128)} %get-tuple-element.198) | copy-start | bytes 37748740 | tf_op jit(solution)/shard_map/while
  92.8 7.6 %copy-start.3 = (bf16[3,1,512,2048]{3,2,1,0:T(8,128)(2,1)S(1)}, bf16[3,1,512,2048]{3,2,1,0:T(8,128)(2,1)}, u32[]{:S(2)}) copy-start(bf16[3,1,512,2048]{3,2,1,0:T(8,128)(2,1)} %get-tuple-element.212) | copy-start | bytes 18874372 | tf_op jit(solution)/shard_map/while
  103.6 4.5 %copy-start.2 = (f32[3,1,512,2048]{3,2,1,0:T(8,128)}, f32[3,1,512,2048]{3,2,1,0:T(8,128)S(1)}, u32[]{:S(2)}) copy-start(f32[3,1,512,2048]{3,2,1,0:T(8,128)S(1)} %fusion.54) | copy-start | bytes 37748740 | tf_op jit(solution)/shard_map/while
  116.7 184.5 %collective-permute-start.4 = (f32[1,512,2048]{2,1,0:T(8,128)}, f32[1,512,2048]{2,1,0:T(8,128)}, u32[]{:S(2)}, u32[]{:S(2)}) collective-permute-start(f32[1,512,2048]{2,1,0:T(8,128)} %get-tuple-element.129), channel_id=1, source_target_pairs={{0,1},{1,0},{2,3},{3,2},{4,5},{5,4},{6,7},{7,6},{8,9},{9,8},{10,11... | collective-permute-start | bytes 12582920 | tf_op jit(solution)/shard_map/ppermute | solution.py:13
  135.6 165.6 %collective-permute-start.5 = (f32[1,512,2048]{2,1,0:T(8,128)}, f32[1,512,2048]{2,1,0:T(8,128)}, u32[]{:S(2)}, u32[]{:S(2)}) collective-permute-start(f32[1,512,2048]{2,1,0:T(8,128)} %get-tuple-element.130), channel_id=1, source_target_pairs={{0,2},{1,3},{2,0},{3,1},{4,6},{5,7},{6,4},{7,5},{8,10},{9,11},{10,... | collective-permute-start | bytes 12582920 | tf_op jit(solution)/shard_map/ppermute | solution.py:13
  137.5 6.6 %collective-permute-start.6 = (f32[512,512]{1,0:T(8,128)S(1)}, f32[512,512]{1,0:T(8,128)S(1)}, u32[]{:S(2)}, u32[]{:S(2)}) collective-permute-start(f32[512,512]{1,0:T(8,128)S(1)} %get-tuple-element.110), channel_id=1, source_target_pairs={{0,1},{1,0},{2,3},{3,2},{4,5},{5,4},{6,7},{7,6},{8,9},{9,8},{10,11... | collective-permute-start | bytes 3145736 | tf_op jit(solution)/shard_map/ppermute | solution.py:98
  144.3 107.1 %collective-permute-start.7 = (f32[512,512]{1,0:T(8,128)S(1)}, f32[512,512]{1,0:T(8,128)S(1)}, u32[]{:S(2)}, u32[]{:S(2)}) collective-permute-start(f32[512,512]{1,0:T(8,128)S(1)} %add.102), channel_id=1, source_target_pairs={{0,2},{1,3},{2,0},{3,1},{4,6},{5,7},{6,4},{7,5},{8,10},{9,11},{10,... | collective-permute-start | bytes 3145736 | tf_op jit(solution)/shard_map/ppermute | solution.py:98
  251.7 48.3 %collective-permute-start.8 = (f32[512,512]{1,0:T(8,128)S(1)}, f32[512,512]{1,0:T(8,128)S(1)}, u32[]{:S(2)}, u32[]{:S(2)}) collective-permute-start(f32[512,512]{1,0:T(8,128)S(1)} %add.103), channel_id=1, source_target_pairs={{0,4},{1,5},{2,6},{3,7},{4,0},{5,1},{6,2},{7,3},{8,12},{9,13},{10,... | collective-permute-start | bytes 3145736 | tf_op jit(solution)/shard_map/ppermute | solution.py:98
  301.2 52.9 %copy-start.4 = (bf16[1,512,2048]{2,1,0:T(8,128)(2,1)S(1)}, bf16[1,512,2048]{2,1,0:T(8,128)(2,1)}, u32[]{:S(2)}) copy-start(bf16[1,512,2048]{2,1,0:T(8,128)(2,1)} %param.7) | copy-start | bytes 6291460
Sparse Core Ops, SparseCore 0:
  301.3 52.7 all-reduce.1
